TPU v7x, 32 devices: a whole 2x2x4 slice. The times are simulated.
32 devices in a mesh: req: 8 (over z, y), tp: 4 (over x, core).
Axes of the slice: x: 2, y: 2, z: 4, core: 2. Of those that a mesh axis runs over, the one named last changes fastest.
Arguments:
- tokens: bfloat16 [16, 256, 2048], P('req'), may hold values from -6 to 6
- attn_gain: float32 [2048], replicated, may hold values from 0.25 to 1.75
- w_query: bfloat16 [2048, 1280], P(None, 'tp'), may hold values from -0.125 to 0.125
- key_value_weight: bfloat16 [2048, 640], replicated, may hold values from -0.125 to 0.125
- w_out: bfloat16 [1280, 2048], P('tp'), may hold values from -0.15625 to 0.15625
- q_gain: float32 [64], replicated, as said below
- k_gain: float32 [64], replicated, as said below
- stored: bfloat16 [8, 5, 2048, 128], P('req'), may hold values from -6 to 6
- continuing: int32 [16], replicated, may hold values from 0 to 1, as said below
- cache_row: int32 [16], replicated, may hold values from -1 to 7, as said below
- cache_len: int32 [16], replicated, may hold values from 0 to 2048, as said below
Outputs:
- layer: bfloat16 [16, 256, 2048], P('req')
- decoding_group_cache: bfloat16 [32, 5, 1152, 128], P('req', None, 'tp')
Inputs may be any that keep to these rules, and one draw needn't show every extreme that they name: `continuing`: exactly 8 requests have 1. `cache_row`: a continuing request's row of stored; every row belongs to exactly one continuing request; -1 for the others. `cache_len`: 1 to 2048 for a continuing request, 2048 for at least one; 0 for the others. `q_gain`: positive. `k_gain`: positive.
All inputs are finite; a program needn't handle non-finite values.
Results may differ from a plain program's by a relative error of at most 0.005.
The roundings to bfloat16 on the way count: a program that leaves them out, or rounds other values in their place, can miss the bound.
Values may be sent and summed in bfloat16 or wider, within the bound.
No kernel may reach another device: no remote copies, remote signals or barrier semaphores. Data moves between devices by JAX's collectives and lax.ppermute only.
A program may use at most 128 MiB of HBM per device.

v0:
```python
import math
import jax
import jax.numpy as jnp
from jax import lax
from jax.sharding import PartitionSpec as P


def swapped(value, axis, apart):
    mask = 2**apart
    pairs = [(source, source ^ mask) for source in range(lax.axis_size(axis))]
    return lax.ppermute(value, axis, pairs)


def normalize(values, gain):
    return values * lax.rsqrt(jnp.mean(values * values, axis=-1, keepdims=True) + 1e-06) * gain


def rotary(values, positions):
    half_dim = values.shape[-1] // 2
    freq = jnp.exp(
        -math.log(10000.0) * jnp.arange(half_dim).astype(jnp.float32) * 2.0 / values.shape[-1]
    )
    angle = positions.astype(jnp.float32)[..., None] * freq
    cosine = jnp.cos(angle)[..., None, :]
    sine = jnp.sin(angle)[..., None, :]
    first_half = values[..., :half_dim]
    second_half = values[..., half_dim:]
    return jnp.concatenate(
        [first_half * cosine - second_half * sine, second_half * cosine + first_half * sine],
        axis=-1,
    )


def attend(query_one, keys_one, allowed, head_dim, new_count, scale):
    scores = (
        jnp.einsum(
            "hqd,hkd->hqk", query_one, keys_one[..., :head_dim], preferred_element_type=jnp.float32
        )
        * scale
    )
    scores = jnp.where(allowed[None], scores, -jnp.inf)
    row_max = jnp.max(scores, axis=-1, keepdims=True)
    weights = jnp.exp(scores - row_max)
    probs = (weights / jnp.sum(weights, axis=-1, keepdims=True)).astype(jnp.bfloat16)
    mixed = jnp.einsum(
        "hqk,hkd->qhd", probs, keys_one[..., head_dim:], preferred_element_type=jnp.float32
    )
    return mixed.astype(jnp.bfloat16).reshape(new_count, query_one.shape[0] * head_dim)


def on_device(
    tokens,
    attn_gain,
    w_query,
    key_value_weight,
    w_out,
    q_gain,
    k_gain,
    stored,
    continuing,
    cache_row,
    cache_len,
):
    tp_count = lax.axis_size("tp")
    req_place = lax.axis_index("req")
    tp_place = lax.axis_index("tp")
    req_dev, new_count, width = tokens.shape
    head_dim = q_gain.shape[0]
    kv_heads = key_value_weight.shape[1] // (2 * head_dim)
    local_heads = w_query.shape[1] // head_dim
    query_group_ratio = local_heads * tp_count // kv_heads
    cache_span = stored.shape[2]
    total_length = cache_span + new_count
    scale = 1.0 / math.sqrt(head_dim)
    relayed = lax.all_to_all(stored, "req", split_axis=2, concat_axis=0, tiled=True)
    live_all = continuing == 1
    rows_all = jnp.where(live_all, cache_row, 0)
    select_chosen = jnp.take(relayed, rows_all, axis=0)
    stored_entries = lax.all_to_all(
        jnp.where(live_all[:, None, None, None], select_chosen, jnp.zeros_like(select_chosen)),
        "req",
        split_axis=0,
        concat_axis=2,
        tiled=True,
    )
    first = req_place * req_dev
    my_live = lax.dynamic_slice_in_dim(continuing, first, req_dev) == 1
    my_len = jnp.where(my_live, lax.dynamic_slice_in_dim(cache_len, first, req_dev), 0)
    position = jnp.arange(cache_span, dtype=jnp.int32)
    stored_entries = jnp.where(
        (position[None, :] < my_len[:, None])[:, None, :, None],
        stored_entries,
        jnp.zeros_like(stored_entries),
    )
    token_rows = tokens.reshape(req_dev * new_count, width)
    normalized_input = normalize(token_rows.astype(jnp.float32), attn_gain).astype(jnp.bfloat16)
    positions = my_len[:, None] + jnp.arange(new_count, dtype=jnp.int32)[None, :]
    query = jnp.dot(normalized_input, w_query, preferred_element_type=jnp.float32).reshape(
        req_dev, new_count, local_heads, head_dim
    )
    query = rotary(normalize(query, q_gain), positions).astype(jnp.bfloat16)
    key_value_rows = jnp.dot(
        normalized_input, key_value_weight, preferred_element_type=jnp.float32
    ).reshape(req_dev, new_count, kv_heads, 2 * head_dim)
    keys_new = rotary(normalize(key_value_rows[..., :head_dim], k_gain), positions)
    fresh = jnp.concatenate([keys_new, key_value_rows[..., head_dim:]], axis=-1).astype(
        jnp.bfloat16
    )
    fresh = jnp.transpose(fresh, (0, 2, 1, 3))
    keys_all = jnp.concatenate([stored_entries, fresh], axis=2)
    head_select = (
        tp_place * local_heads + jnp.arange(local_heads, dtype=jnp.int32)
    ) // query_group_ratio
    query_index = jnp.arange(new_count, dtype=jnp.int32)[:, None]
    key_index = jnp.arange(total_length, dtype=jnp.int32)[None, :]
    outputs = []
    for number in range(req_dev):
        query_one = jnp.transpose(query[number], (1, 0, 2))
        chosen = jnp.take(keys_all[number], head_select, axis=0)
        allowed = jnp.where(
            key_index < cache_span,
            key_index < my_len[number],
            key_index - cache_span <= query_index,
        )
        mixed = attend(query_one, chosen, allowed, head_dim, new_count, scale)
        outputs.append(mixed)
    mixed_all = jnp.concatenate(outputs, axis=0)
    summed = lax.psum(jnp.dot(mixed_all, w_out, preferred_element_type=jnp.float32), "tp")
    layer = (token_rows.astype(jnp.float32) + summed).astype(jnp.bfloat16)
    layer = layer.reshape(req_dev, new_count, width)
    padded_tokens = jnp.concatenate(
        [stored_entries, jnp.zeros((req_dev, kv_heads, new_count, 2 * head_dim), jnp.bfloat16)],
        axis=2,
    )
    whole = jax.vmap(
        lambda padded_one, fresh_one, offset: lax.dynamic_update_slice_in_dim(
            padded_one, fresh_one, offset, 1
        )
    )(padded_tokens, fresh, my_len)
    half_span = total_length // 2
    segment = half_span // tp_count
    pair_side = req_place % 2
    kept_half = lax.dynamic_slice_in_dim(
        whole, pair_side * half_span + tp_place * segment, segment, 2
    )
    sent_half = lax.dynamic_slice_in_dim(
        whole, (1 - pair_side) * half_span + tp_place * segment, segment, 2
    )
    partner = swapped(sent_half, "req", 0)
    decoding_group_cache = jnp.where(
        pair_side == 0,
        jnp.concatenate([kept_half, partner], axis=0),
        jnp.concatenate([partner, kept_half], axis=0),
    )
    return (layer, decoding_group_cache)


def solution(mesh):
    return jax.shard_map(
        on_device,
        mesh=mesh,
        in_specs=(
            P("req", None, None),
            P(),
            P(None, "tp"),
            P(),
            P("tp", None),
            P(),
            P(),
            P("req", None, None, None),
            P(),
            P(),
            P(),
        ),
        out_specs=(P("req", None, None), P("req", None, "tp", None)),
        check_vma=False,
    )
```

profile of v0, /device:TPU:0, one launch (start us, length us, event | category | flops | bytes accessed | tf_op | source)
XLA Modules:
  0.0 405.0 jit_solution(1439324511392412007)
XLA Ops:
  7.2 5.2 %copy.40 = bf16[1,5,2048,128]{3,1,0,2:T(8,128)(2,1)} copy(bf16[1,5,2048,128]{3,2,1,0:T(8,128)(2,1)} %param.20) | data formatting | bytes 5242880 | tf_op args[7]
  12.4 7.4 %all-to-all-start = ((bf16[1,5,2048,128]{3,1,0,2:T(8,128)(2,1)}), bf16[1,5,2048,128]{3,1,0,2:T(8,128)(2,1)}, u32[]{:S(2)}, u32[]{:S(2)}) async-start(bf16[1,5,2048,128]{3,1,0,2:T(8,128)(2,1)} %copy.40), calls=%async_computation | async-start | bytes 8388608 | tf_op jit(solution)/shard_map/all_to_all | solution.py:75
  19.9 93.2 %all-to-all-done = bf16[1,5,2048,128]{3,1,0,2:T(8,128)(2,1)} async-done(((bf16[1,5,2048,128]{3,1,0,2:T(8,128)(2,1)}), bf16[1,5,2048,128]{3,1,0,2:T(8,128)(2,1)}, u32[]{:S(2)}, u32[]{:S(2)}) %all-to-all-start) | async-done | bytes 2621472 | tf_op jit(solution)/shard_map/all_to_all | solution.py:75
  113.1 4.4 %copy.54 = bf16[1,5,8,256,128]{4,3,1,2,0:T(8,128)(2,1)} copy(bf16[1,5,8,256,128]{4,1,3,2,0:T(8,128)(2,1)} %bitcast.1) | data formatting | bytes 5242880 | tf_op jit(solution)/shard_map/all_to_all | solution.py:75
  117.6 5.3 %gather_fusion = bf16[16,5,256,128]{3,2,1,0:T(8,128)(2,1)} fusion(bf16[8,5,256,128]{3,2,1,0:T(8,128)(2,1)} %bitcast.95, s32[1024]{0:T(1024)S(1)} %pad_clamp_fusion.1), kind=kCustom, calls=%fused_computation.2 | custom fusion | bytes 10485824 | tf_op jit(solution)/shard_map/jit(_take)/gather | solution.py:78
  122.9 5.5 %select_select_fusion = bf16[16,5,256,128]{3,2,1,0:T(8,128)(2,1)} fusion(bf16[16,5,256,128]{3,2,1,0:T(8,128)(2,1)} %gather_fusion, pred[16]{0:T(512)(128)(4,1)S(1)} %get-tuple-element.41, pred[16]{0:T(512)(128)(4,1)S(1)} %get-tuple-element.65), kind=kLoop, calls=%fused_computation.27 | loop fusion | flops 5242880 | bytes 10485792 | tf_op jit(solution)/shard_map/jit(_where)/select_n | solution.py:80
  128.3 4.6 %all-to-all-start.1 = ((bf16[16,5,256,128]{3,2,1,0:T(8,128)(2,1)}), bf16[16,5,256,128]{3,2,1,0:T(8,128)(2,1)}, u32[]{:S(2)}, u32[]{:S(2)}) async-start(bf16[16,5,256,128]{3,2,1,0:T(8,128)(2,1)} %select_select_fusion), calls=%async_computation.1 | async-start | bytes 10485760 | tf_op jit(solution)/shard_map/all_to_all | solution.py:79
  133.2 4.6 %copy.44 = bf16[2048,640]{0,1:T(8,128)(2,1)} copy(bf16[2048,640]{1,0:T(8,128)(2,1)} %param.16) | data formatting | bytes 5242880 | tf_op args[3]
  151.3 96.6 %all-to-all-done.1 = bf16[16,5,256,128]{3,2,1,0:T(8,128)(2,1)} async-done(((bf16[16,5,256,128]{3,2,1,0:T(8,128)(2,1)}), bf16[16,5,256,128]{3,2,1,0:T(8,128)(2,1)}, u32[]{:S(2)}, u32[]{:S(2)}) %all-to-all-start.1) | async-done | bytes 5242912 | tf_op jit(solution)/shard_map/all_to_all | solution.py:79
  256.1 4.6 %gather_fusion.1 = bf16[5,2304,128]{2,1,0:T(8,128)(2,1)} fusion(bf16[5,2304,128]{2,1,0:T(8,128)(2,1)} %get-tuple-element.49, s32[1024]{0:T(1024)S(1)} %pad_clamp_fusion), kind=kCustom, calls=%fused_computation.clone | custom fusion | bytes 5898260 | tf_op jit(solution)/shard_map/jit(_take)/gather | solution.py:119
  260.7 5.4 %copy.46 = bf16[5,2304,128]{1,2,0:T(8,128)(2,1)} copy(bf16[5,2304,128]{2,1,0:T(8,128)(2,1)} %gather_fusion.1) | data formatting | bytes 5898240 | tf_op jit(solution)/shard_map/jit(_take)/gather | solution.py:119
  266.1 4.6 %gather_fusion.2 = bf16[5,2304,128]{2,1,0:T(8,128)(2,1)} fusion(bf16[5,2304,128]{2,1,0:T(8,128)(2,1)} %get-tuple-element.50, s32[1024]{0:T(1024)S(1)} %pad_clamp_fusion), kind=kCustom, calls=%fused_computation.1.clone | custom fusion | bytes 5898260 | tf_op jit(solution)/shard_map/jit(_take)/gather | solution.py:119
  270.8 5.4 %copy.47 = bf16[5,2304,128]{1,2,0:T(8,128)(2,1)} copy(bf16[5,2304,128]{2,1,0:T(8,128)(2,1)} %gather_fusion.2) | data formatting | bytes 5898240 | tf_op jit(solution)/shard_map/jit(_take)/gather | solution.py:119
  276.2 5.8 %broadcast_select_fusion.1 = (bf16[5,2304,128]{1,2,0:T(8,128)(2,1)}, bf16[5,2304,128]{1,2,0:T(8,128)(2,1)}) fusion(bf16[5,2304,128]{1,2,0:T(8,128)(2,1)} %copy.46, pred[5]{0:T(512)(128)(4,1)S(1)} %compare_and_fusion, bf16[5,2304,128]{1,2,0:T(8,128)(2,1)} %copy.47), kind=kLoop, calls=%fused_computation.37 | loop fusion | flops 2949120 | bytes 11796485 | tf_op jit(solution)/shard_map/jit(_take)/select_n | solution.py:119
  282.0 5.2 %fusion.90 = f32[5,256]{1,0:T(8,128)S(1)} fusion(pred[256,2304]{1,0:T(8,128)(4,1)S(1)} %get-tuple-element.58, bf16[5,2304,128]{1,2,0:T(8,128)(2,1)} %get-tuple-element.62, bf16[2,256,5,32]{1,3,2,0:T(8,128)(2,1)S(1)} %get-tuple-element.52, bf16[2,256,5,32]{1,3,2,0:T(8,128)(2,1)S(1)} %get-tuple-element.51), kind=kOutput, calls=%fused_computation.119 | convolution fusion | flops 389613824 | bytes 2397184 | tf_op jit(solution)/shard_map/sub | solution.py:43
  287.2 7.0 %fusion.37 = bf16[5,64,256]{2,1,0:T(8,128)(2,1)} fusion(f32[5,256]{1,0:T(8,128)S(1)} %fusion.90, bf16[5,2304,128]{1,2,0:T(8,128)(2,1)} %get-tuple-element.62, pred[256,2304]{1,0:T(8,128)(4,1)S(1)} %get-tuple-element.58, bf16[2,256,5,32]{1,3,2,0:T(8,128)(2,1)S(1)} %get-tuple-element.52, bf16[2,256,5,32]{1,3,2,0:T(8,128)(2,1)S(1)} %get-tuple-element.51), kind=kOutput, calls=%fused_computation.54 | convolution fusion | flops 770133504 | bytes 4035584 | tf_op jit(solution)/shard_map/hqk,hkd->qhd/dot_general | solution.py:45
  294.2 5.5 %fusion.95 = f32[5,256]{1,0:T(8,128)S(1)} fusion(pred[256,2304]{1,0:T(8,128)(4,1)S(1)} %get-tuple-element.57, bf16[5,2304,128]{1,2,0:T(8,128)(2,1)} %get-tuple-element.61, bf16[2,256,5,32]{1,3,2,0:T(8,128)(2,1)S(1)} %get-tuple-element.51, bf16[2,256,5,32]{1,3,2,0:T(8,128)(2,1)S(1)} %get-tuple-element.52), kind=kOutput, calls=%fused_computation.120 | convolution fusion | flops 389613824 | bytes 2397184 | tf_op jit(solution)/shard_map/sub | solution.py:43
  299.6 6.3 %fusion.40 = bf16[5,64,256]{2,1,0:T(8,128)(2,1)S(1)} fusion(f32[5,256]{1,0:T(8,128)S(1)} %fusion.95, bf16[5,2304,128]{1,2,0:T(8,128)(2,1)} %get-tuple-element.61, pred[256,2304]{1,0:T(8,128)(4,1)S(1)} %get-tuple-element.57, bf16[2,256,5,32]{1,3,2,0:T(8,128)(2,1)S(1)} %get-tuple-element.51, bf16[2,256,5,32]{1,3,2,0:T(8,128)(2,1)S(1)} %get-tuple-element.52), kind=kOutput, calls=%fused_computation.55 | convolution fusion | flops 770133504 | bytes 4035584 | tf_op jit(solution)/shard_map/hqk,hkd->qhd/dot_general | solution.py:45
  310.1 5.6 %concatenate.30 = bf16[2,5,2304,128]{3,2,1,0:T(8,128)(2,1)} pad(bf16[2,5,2048,128]{3,2,1,0:T(8,128)(2,1)} %copy-done.1, bf16[]{:T(256)} %constant.52.clone.1), padding=0_0x0_0x0_256x0_0 | pad | bytes 11141122 | tf_op jit(solution)/shard_map/concatenate | solution.py:131
  315.7 24.9 %while.1 = (s32[]{:T(128)}, bf16[2,5,2304,128]{3,2,1,0:T(8,128)(2,1)}, s32[2,4]{1,0:T(2,128)S(1)}, bf16[2,5,256,128]{3,2,1,0:T(8,128)(2,1)S(1)}, s32[]{:T(128)}, /*index=5*/s32[4]{0:T(128)S(1)}, s32[]{:T(128)}) while((s32[]{:T(128)}, bf16[2,5,2304,128]{3,2,1,0:T(8,128)(2,1)}, s32[2,4]{1,0:T(2,128)S(1)}, bf16[2,5,256,128]{3,2,1,0:T(8,128)(2,1)S(1)}, ...), condition=%wide.while_cond, body=%wide.while_body.sunk | while | flops 163869 | bytes 1638603 | solution.py:136
  322.5 5.6 %dynamic-update-slice.3 = bf16[2,5,2304,128]{3,2,1,0:T(8,128)(2,1)} dynamic-update-slice(bf16[2,5,2304,128]{3,2,1,0:T(8,128)(2,1)} %get-tuple-element.113, bf16[1,5,256,128]{3,2,1,0:T(8,128)(2,1)S(1)} %dynamic-slice_select_fusion.2, s32[]{:T(128)} %bitcast.89, s32[]{:T(128)} %constant.38.clone.1..sunk, s32[]{:T(128)} %bitcast.90, s32[]{:T(128)} %constant.38.clone.1..sunk) | dynamic-update-slice | bytes 655364 | tf_op jit(solution)/shard_map/vmap(vmap())/scatter
  335.0 5.6 %dynamic-update-slice.3 = bf16[2,5,2304,128]{3,2,1,0:T(8,128)(2,1)} dynamic-update-slice(bf16[2,5,2304,128]{3,2,1,0:T(8,128)(2,1)} %get-tuple-element.113, bf16[1,5,256,128]{3,2,1,0:T(8,128)(2,1)S(1)} %dynamic-slice_select_fusion.2, s32[]{:T(128)} %bitcast.89, s32[]{:T(128)} %constant.38.clone.1..sunk, s32[]{:T(128)} %bitcast.90, s32[]{:T(128)} %constant.38.clone.1..sunk) | dynamic-update-slice | bytes 655364 | tf_op jit(solution)/shard_map/vmap(vmap())/scatter
  344.9 15.9 %collective-permute-done = bf16[2,5,288,128]{3,2,1,0:T(8,128)(2,1)} collective-permute-done((bf16[2,5,288,128]{3,2,1,0:T(8,128)(2,1)}, bf16[2,5,288,128]{3,2,1,0:T(8,128)(2,1)}, u32[]{:S(2)}, u32[]{:S(2)}) %collective-permute-start) | collective-permute-done | bytes 737312 | tf_op jit(solution)/shard_map/ppermute | solution.py:11
  364.0 30.0 %all-reduce.3.cloned.1.call-done = f32[512,2048]{1,0:T(8,128)} async-done(((f32[512,2048]{1,0:T(8,128)}), f32[512,2048]{1,0:T(8,128)}) %all-reduce.3.cloned.1.call-update) | async-done | bytes 4194320 | tf_op jit(solution)/shard_map/psum | solution.py:128
  (82 shorter events, 51.2 us)
Async XLA Ops:
  7.2 298.8 %copy-start = (bf16[320,2048]{1,0:T(8,128)(2,1)S(1)}, bf16[320,2048]{1,0:T(8,128)(2,1)}, u32[]{:S(2)}) copy-start(bf16[320,2048]{1,0:T(8,128)(2,1)} %param.17) | copy-start | bytes 3932164
  12.4 7.4 %copy-start.9 = (s32[16]{0:T(128)S(1)}, s32[16]{0:T(128)}, u32[]{:S(2)}) copy-start(s32[16]{0:T(128)} %param.21) | copy-start | bytes 196
  12.4 7.4 %copy-start.12 = (s32[16]{0:T(128)S(1)}, s32[16]{0:T(128)}, u32[]{:S(2)}) copy-start(s32[16]{0:T(128)} %param.22) | copy-start | bytes 196
  12.4 100.7 %all-to-all-start = ((bf16[1,5,2048,128]{3,1,0,2:T(8,128)(2,1)}), bf16[1,5,2048,128]{3,1,0,2:T(8,128)(2,1)}, u32[]{:S(2)}, u32[]{:S(2)}) async-start(bf16[1,5,2048,128]{3,1,0,2:T(8,128)(2,1)} %copy.40), calls=%async_computation | async-start | bytes 8388608 | tf_op jit(solution)/shard_map/all_to_all | solution.py:75
  128.3 119.6 %all-to-all-start.1 = ((bf16[16,5,256,128]{3,2,1,0:T(8,128)(2,1)}), bf16[16,5,256,128]{3,2,1,0:T(8,128)(2,1)}, u32[]{:S(2)}, u32[]{:S(2)}) async-start(bf16[16,5,256,128]{3,2,1,0:T(8,128)(2,1)} %select_select_fusion), calls=%async_computation.1 | async-start | bytes 10485760 | tf_op jit(solution)/shard_map/all_to_all | solution.py:79
  133.0 4.8 %copy-start.2 = (bf16[2,256,2048]{2,1,0:T(8,128)(2,1)S(1)}, bf16[2,256,2048]{2,1,0:T(8,128)(2,1)}, u32[]{:S(2)}) copy-start(bf16[2,256,2048]{2,1,0:T(8,128)(2,1)} %param.13) | copy-start | bytes 6291460
  133.0 261.0 %all-reduce.3.cloned.1.call-start = ((), (), s32[]{:S(2)}) async-start(), calls=%async_computation.2 | async-start | bytes 8388608 | tf_op jit(solution)/shard_map/psum | solution.py:128
  133.2 5.1 %copy-start.15 = (f32[2048]{0:T(1024)S(1)}, f32[2048]{0:T(1024)}, u32[]{:S(2)}) copy-start(f32[2048]{0:T(1024)} %param.14) | copy-start | bytes 24580
  138.3 5.2 %copy-start.13 = (s32[16]{0:T(128)S(1)}, s32[16]{0:T(128)}, u32[]{:S(2)}) copy-start(s32[16]{0:T(128)} %param.23) | copy-start | bytes 196
  141.7 1.1 copy-start.4
  144.9 2.8 copy-start.5
  144.9 2.8 copy-start.10
  144.9 2.8 copy-start.11
  147.3 1.0 copy-start.6
  252.0 4.1 %copy-start.1 = (bf16[2,5,2048,128]{3,2,1,0:T(8,128)(2,1)}, bf16[2,5,2048,128]{3,2,1,0:T(8,128)(2,1)S(1)}, u32[]{:S(2)}) copy-start(bf16[2,5,2048,128]{3,2,1,0:T(8,128)(2,1)S(1)} %bitcast_select_fusion) | copy-start | bytes 15728644
  299.6 6.4 %copy-start.7 = (bf16[5,64,256]{2,1,0:T(8,128)(2,1)S(1)}, bf16[5,64,256]{2,1,0:T(8,128)(2,1)}, u32[]{:S(2)}) copy-start(bf16[5,64,256]{2,1,0:T(8,128)(2,1)} %fusion.37) | copy-start | bytes 491524
  309.3 0.7 copy-start.14
  310.1 5.6 %copy-start.8 = (s32[4]{0:T(128)S(1)}, s32[4]{0:T(128)}, u32[]{:S(2)}) copy-start(s32[4]{0:T(128)} %constant.238) | copy-start | bytes 52
  340.5 53.4 %copy-start.3 = (bf16[2,256,2048]{2,1,0:T(8,128)(2,1)S(1)}, bf16[2,256,2048]{2,1,0:T(8,128)(2,1)}, u32[]{:S(2)}) copy-start(bf16[2,256,2048]{2,1,0:T(8,128)(2,1)} %param.13) | copy-start | bytes 6291460
  343.3 17.6 %collective-permute-start = (bf16[2,5,288,128]{3,2,1,0:T(8,128)(2,1)}, bf16[2,5,288,128]{3,2,1,0:T(8,128)(2,1)}, u32[]{:S(2)}, u32[]{:S(2)}) collective-permute-start(bf16[2,5,288,128]{3,2,1,0:T(8,128)(2,1)} %get-tuple-element.48), channel_id=1, source_target_pairs={{0,4},{4,0},{8,12},{12,8},{16,20},{20,16},{24,28},{28,24},{1,5},{5... | collective-permute-start | bytes 2211848 | tf_op jit(solution)/shard_map/ppermute | solution.py:11
Sparse Core Ops, SparseCore 0:
  309.4 84.5 all-reduce.2
where the time goes:
time: 407 us; the launch traced here: 405 us
  waiting for transfers between devices  236 us (58%)
  local copies, waits for them, and re-layouts  66.8 us (16%)
  other arithmetic  41.1 us (10%)
  matrix products  33 us (8%)
  between operations  14.3 us (4%)
  starting transfers between devices  13.9 us (3%)
    all_to_all x1, waiting for transfers between devices, on_device(): lax.all_to_all(jnp.where(live_all[:, None, None, None], select_chosen, jn...  96.6 us
    all_to_all x1, waiting for transfers between devices, on_device(): lax.all_to_all(stored, 'req', split_axis=2, concat_axis=0, tiled=True)  93.2 us
    psum x1, waiting for transfers between devices, on_device(): lax.psum(jnp.dot(mixed_all, w_out, preferred_element_type=jnp.float32), '...  30 us
    gather x4, local copies, waits for them, and re-layouts, on_device(): chosen = jnp.take(keys_all[number], head_select, axis=0)  20.1 us
    ppermute x1, waiting for transfers between devices, swapped(): return lax.ppermute(value, axis, pairs)  15.9 us
    dot_general x2, matrix products, attend(): jnp.einsum('hqk,hkd->qhd', probs, keys_one[..., head_dim:], preferred_ele...  13.3 us
    scatter x6, local copies, waits for them, and re-layouts  12.4 us
    scatter x4, other arithmetic  12.4 us
  transfers between devices with their start and end apart: 4, of which 4 were waited for; matrix products, arithmetic and copies ran while one was open for 13% of the time, Pallas kernels for 0%

commit v1 on v0

--- a/solution.py
+++ b/solution.py
@@ -72,7 +72,29 @@
     cache_span = stored.shape[2]
     total_length = cache_span + new_count
     scale = 1.0 / math.sqrt(head_dim)
-    relayed = lax.all_to_all(stored, "req", split_axis=2, concat_axis=0, tiled=True)
+
+    def treat_inputs_in(obj):
+        wide_out, x_new = (lax.axis_size("req"), lax.axis_index("req"))
+        current_block = obj.shape[2] // wide_out
+        r1 = list(obj.shape)
+        r1[2] = current_block
+        tall = r1[0]
+        r1[0] = tall * wide_out
+        now = jnp.zeros(r1, obj.dtype)
+        c = 0
+        while c < wide_out:
+            far_arr = lax.dynamic_slice_in_dim(
+                obj, (x_new ^ c) * current_block, current_block, axis=2
+            )
+            if c:
+                far_arr = lax.ppermute(
+                    far_arr, "req", tuple(((pp, pp ^ c) for pp in range(wide_out)))
+                )
+            now = lax.dynamic_update_slice_in_dim(now, far_arr, (x_new ^ c) * tall, axis=0)
+            c += 1
+        return now
+
+    relayed = treat_inputs_in(stored)
     live_all = continuing == 1
     rows_all = jnp.where(live_all, cache_row, 0)
     select_chosen = jnp.take(relayed, rows_all, axis=0)

time: 407 us -> 364 us (0.89)
  waiting for transfers between devices: 236 us -> 175 us
  starting transfers between devices: 13.9 us -> 27.6 us
  local copies, waits for them, and re-layouts: 66.8 us -> 71.1 us
    all_to_all x1 -> x0, waiting for transfers between devices: 93.2 us -> none  [on_device(): lax.all_to_all(stored, 'req', split_axis=2, concat_axis=0, tiled=True)]
    ppermute x0 -> x7, waiting for transfers between devices: none -> 32 us  [treat_inputs_in(): lax.ppermute(far_arr, 'req', tuple(((pp, pp ^ c) for pp in range(wide_out...]
    ppermute x0 -> x7, starting transfers between devices: none -> 13.6 us  [treat_inputs_in(): lax.ppermute(far_arr, 'req', tuple(((pp, pp ^ c) for pp in range(wide_out...]
    dynamic_update_slice x0 -> x7, local copies, waits for them, and re-layouts: none -> 10.1 us  [treat_inputs_in(): lax.dynamic_update_slice_in_dim(now, far_arr, (x_new ^ c) * tall, axis=0)]
    all_to_all x1, starting transfers between devices: 4.65 us -> 13.5 us  [on_device(): lax.all_to_all(jnp.where(live_all[:, None, None, None], select_chosen, jn...]
    all_to_all x1 -> x0, starting transfers between devices: 7.41 us -> none  [on_device(): lax.all_to_all(stored, 'req', split_axis=2, concat_axis=0, tiled=True)]
    unnamed x36 -> x37, local copies, waits for them, and re-layouts: 11.8 us -> 6.92 us
    all_to_all x1 -> x0, local copies, waits for them, and re-layouts: 4.45 us -> none  [on_device(): lax.all_to_all(stored, 'req', split_axis=2, concat_axis=0, tiled=True)]
  transfers between devices with their start and end apart: 4 -> 10, of which waited for: 4 -> 7; matrix products, arithmetic and copies ran while one was open for 13% -> 17% of each run, Pallas kernels for 0% -> 0%
where the time goes in v1:
time: 364 us; the launch traced here: 362 us
  waiting for transfers between devices  175 us (48%)
  local copies, waits for them, and re-layouts  71.1 us (20%)
  other arithmetic  41.2 us (11%)
  matrix products  32.9 us (9%)
  starting transfers between devices  27.6 us (8%)
  between operations  14.4 us (4%)
    all_to_all x1, waiting for transfers between devices, on_device(): lax.all_to_all(jnp.where(live_all[:, None, None, None], select_chosen, jn...  97.1 us
    ppermute x7, waiting for transfers between devices, treat_inputs_in(): lax.ppermute(far_arr, 'req', tuple(((pp, pp ^ c) for pp in range(wide_out...  32 us
    psum x1, waiting for transfers between devices, on_device(): lax.psum(jnp.dot(mixed_all, w_out, preferred_element_type=jnp.float32), '...  29.6 us
    gather x4, local copies, waits for them, and re-layouts, on_device(): chosen = jnp.take(keys_all[number], head_select, axis=0)  20.1 us
    ppermute x1, waiting for transfers between devices, swapped(): return lax.ppermute(value, axis, pairs)  15.9 us
    ppermute x7, starting transfers between devices, treat_inputs_in(): lax.ppermute(far_arr, 'req', tuple(((pp, pp ^ c) for pp in range(wide_out...  13.6 us
    all_to_all x1, starting transfers between devices, on_device(): lax.all_to_all(jnp.where(live_all[:, None, None, None], select_chosen, jn...  13.5 us
    dot_general x2, matrix products, attend(): jnp.einsum('hqk,hkd->qhd', probs, keys_one[..., head_dim:], preferred_ele...  13.3 us
  transfers between devices with their start and end apart: 10, of which 7 were waited for; matrix products, arithmetic and copies ran while one was open for 17% of the time, Pallas kernels for 0%

profile of v1, /device:TPU:0, one launch (start us, length us, event | category | flops | bytes accessed | tf_op | source)
XLA Modules:
  0.0 361.9 jit_solution(6974599988811653636)
XLA Ops:
  27.2 10.3 %collective-permute-done.1 = bf16[1,5,256,128]{3,2,1,0:T(8,128)(2,1)} collective-permute-done((bf16[1,5,256,128]{3,2,1,0:T(8,128)(2,1)S(1)}, bf16[1,5,256,128]{3,2,1,0:T(8,128)(2,1)}, u32[]{:S(2)}, u32[]{:S(2)}) %collective-permute-start.1) | collective-permute-done | bytes 327712 | tf_op jit(solution)/shard_map/ppermute | solution.py:90
  45.6 17.7 %collective-permute-done.4 = bf16[1,5,256,128]{3,2,1,0:T(8,128)(2,1)} collective-permute-done((bf16[1,5,256,128]{3,2,1,0:T(8,128)(2,1)S(1)}, bf16[1,5,256,128]{3,2,1,0:T(8,128)(2,1)}, u32[]{:S(2)}, u32[]{:S(2)}) %collective-permute-start.4) | collective-permute-done | bytes 327712 | tf_op jit(solution)/shard_map/ppermute | solution.py:90
  66.6 5.3 %gather_fusion = bf16[16,5,256,128]{3,2,1,0:T(8,128)(2,1)} fusion(bf16[8,5,256,128]{3,2,1,0:T(8,128)(2,1)} %constant_dynamic-update-slice_fusion, s32[1024]{0:T(1024)S(1)} %pad_clamp_fusion.1), kind=kCustom, calls=%fused_computation.2 | custom fusion | bytes 10485824 | tf_op jit(solution)/shard_map/jit(_take)/gather | solution.py:100
  71.9 5.5 %select_select_fusion = bf16[16,5,256,128]{3,2,1,0:T(8,128)(2,1)} fusion(bf16[16,5,256,128]{3,2,1,0:T(8,128)(2,1)} %gather_fusion, pred[16]{0:T(512)(128)(4,1)S(1)} %get-tuple-element.29, pred[16]{0:T(512)(128)(4,1)S(1)} %get-tuple-element.61), kind=kLoop, calls=%fused_computation.27 | loop fusion | flops 5242880 | bytes 10485792 | tf_op jit(solution)/shard_map/jit(_where)/select_n | solution.py:102
  77.3 13.5 %all-to-all-start = ((bf16[16,5,256,128]{3,2,1,0:T(8,128)(2,1)}), bf16[16,5,256,128]{3,2,1,0:T(8,128)(2,1)}, u32[]{:S(2)}, u32[]{:S(2)}) async-start(bf16[16,5,256,128]{3,2,1,0:T(8,128)(2,1)} %select_select_fusion), calls=%async_computation | async-start | bytes 10485760 | tf_op jit(solution)/shard_map/all_to_all | solution.py:101
  90.9 4.6 %copy.18 = bf16[2048,640]{0,1:T(8,128)(2,1)} copy(bf16[2048,640]{1,0:T(8,128)(2,1)} %param.16) | data formatting | bytes 5242880 | tf_op args[3]
  109.0 97.1 %all-to-all-done = bf16[16,5,256,128]{3,2,1,0:T(8,128)(2,1)} async-done(((bf16[16,5,256,128]{3,2,1,0:T(8,128)(2,1)}), bf16[16,5,256,128]{3,2,1,0:T(8,128)(2,1)}, u32[]{:S(2)}, u32[]{:S(2)}) %all-to-all-start) | async-done | bytes 5242912 | tf_op jit(solution)/shard_map/all_to_all | solution.py:101
  210.1 4.1 %fusion.14 = (bf16[5,2304,128]{2,1,0:T(8,128)(2,1)}, bf16[5,2304,128]{2,1,0:T(8,128)(2,1)}) fusion(bf16[2,5,2048,128]{3,2,1,0:T(8,128)(2,1)S(1)} %bitcast_select_fusion, bf16[2,5,256,128]{3,2,1,0:T(8,128)(2,1)S(1)} %copy.19), kind=kLoop, calls=%fused_computation.33 | loop fusion | flops 11796480 | bytes 11796480 | tf_op jit(solution)/shard_map/squeeze | solution.py:141
  214.3 4.6 %gather_fusion.1 = bf16[5,2304,128]{2,1,0:T(8,128)(2,1)} fusion(bf16[5,2304,128]{2,1,0:T(8,128)(2,1)} %get-tuple-element.37, s32[1024]{0:T(1024)S(1)} %pad_clamp_fusion), kind=kCustom, calls=%fused_computation.clone | custom fusion | bytes 5898260 | tf_op jit(solution)/shard_map/jit(_take)/gather | solution.py:141
  218.9 5.4 %copy.20 = bf16[5,2304,128]{1,2,0:T(8,128)(2,1)} copy(bf16[5,2304,128]{2,1,0:T(8,128)(2,1)} %gather_fusion.1) | data formatting | bytes 5898240 | tf_op jit(solution)/shard_map/jit(_take)/gather | solution.py:141
  224.3 4.6 %gather_fusion.2 = bf16[5,2304,128]{2,1,0:T(8,128)(2,1)} fusion(bf16[5,2304,128]{2,1,0:T(8,128)(2,1)} %get-tuple-element.38, s32[1024]{0:T(1024)S(1)} %pad_clamp_fusion), kind=kCustom, calls=%fused_computation.1.clone | custom fusion | bytes 5898260 | tf_op jit(solution)/shard_map/jit(_take)/gather | solution.py:141
  228.9 5.4 %copy.21 = bf16[5,2304,128]{1,2,0:T(8,128)(2,1)} copy(bf16[5,2304,128]{2,1,0:T(8,128)(2,1)} %gather_fusion.2) | data formatting | bytes 5898240 | tf_op jit(solution)/shard_map/jit(_take)/gather | solution.py:141
  234.3 5.9 %broadcast_select_fusion.1 = (bf16[5,2304,128]{1,2,0:T(8,128)(2,1)}, bf16[5,2304,128]{1,2,0:T(8,128)(2,1)}) fusion(bf16[5,2304,128]{1,2,0:T(8,128)(2,1)} %copy.20, pred[5]{0:T(512)(128)(4,1)S(1)} %compare_and_fusion, bf16[5,2304,128]{1,2,0:T(8,128)(2,1)} %copy.21), kind=kLoop, calls=%fused_computation.37 | loop fusion | flops 2949120 | bytes 11796485 | tf_op jit(solution)/shard_map/jit(_take)/select_n | solution.py:141
  240.2 5.2 %fusion.90 = f32[5,256]{1,0:T(8,128)S(1)} fusion(pred[256,2304]{1,0:T(8,128)(4,1)S(1)} %get-tuple-element.54, bf16[5,2304,128]{1,2,0:T(8,128)(2,1)} %get-tuple-element.58, bf16[2,256,5,32]{1,3,2,0:T(8,128)(2,1)S(1)} %get-tuple-element.48, bf16[2,256,5,32]{1,3,2,0:T(8,128)(2,1)S(1)} %get-tuple-element.47), kind=kOutput, calls=%fused_computation.133 | convolution fusion | flops 389613824 | bytes 2397184 | tf_op jit(solution)/shard_map/sub | solution.py:43
  245.4 7.0 %fusion.37 = bf16[5,64,256]{2,1,0:T(8,128)(2,1)} fusion(f32[5,256]{1,0:T(8,128)S(1)} %fusion.90, bf16[5,2304,128]{1,2,0:T(8,128)(2,1)} %get-tuple-element.58, pred[256,2304]{1,0:T(8,128)(4,1)S(1)} %get-tuple-element.54, bf16[2,256,5,32]{1,3,2,0:T(8,128)(2,1)S(1)} %get-tuple-element.48, bf16[2,256,5,32]{1,3,2,0:T(8,128)(2,1)S(1)} %get-tuple-element.47), kind=kOutput, calls=%fused_computation.53 | convolution fusion | flops 770133504 | bytes 4035584 | tf_op jit(solution)/shard_map/hqk,hkd->qhd/dot_general | solution.py:45
  252.4 5.4 %fusion.95 = f32[5,256]{1,0:T(8,128)S(1)} fusion(pred[256,2304]{1,0:T(8,128)(4,1)S(1)} %get-tuple-element.53, bf16[5,2304,128]{1,2,0:T(8,128)(2,1)} %get-tuple-element.57, bf16[2,256,5,32]{1,3,2,0:T(8,128)(2,1)S(1)} %get-tuple-element.47, bf16[2,256,5,32]{1,3,2,0:T(8,128)(2,1)S(1)} %get-tuple-element.48), kind=kOutput, calls=%fused_computation.134 | convolution fusion | flops 389613824 | bytes 2397184 | tf_op jit(solution)/shard_map/sub | solution.py:43
  257.8 6.3 %fusion.40 = bf16[5,64,256]{2,1,0:T(8,128)(2,1)S(1)} fusion(f32[5,256]{1,0:T(8,128)S(1)} %fusion.95, bf16[5,2304,128]{1,2,0:T(8,128)(2,1)} %get-tuple-element.57, pred[256,2304]{1,0:T(8,128)(4,1)S(1)} %get-tuple-element.53, bf16[2,256,5,32]{1,3,2,0:T(8,128)(2,1)S(1)} %get-tuple-element.47, bf16[2,256,5,32]{1,3,2,0:T(8,128)(2,1)S(1)} %get-tuple-element.48), kind=kOutput, calls=%fused_computation.54 | convolution fusion | flops 770133504 | bytes 4035584 | tf_op jit(solution)/shard_map/hqk,hkd->qhd/dot_general | solution.py:45
  268.2 5.6 %concatenate.30 = bf16[2,5,2304,128]{3,2,1,0:T(8,128)(2,1)} pad(bf16[2,5,2048,128]{3,2,1,0:T(8,128)(2,1)} %copy-done.1, bf16[]{:T(256)} %constant.35.clone.1), padding=0_0x0_0x0_256x0_0 | pad | bytes 11141122 | tf_op jit(solution)/shard_map/concatenate | solution.py:153
  273.9 25.3 %while.1 = (s32[]{:T(128)}, bf16[2,5,2304,128]{3,2,1,0:T(8,128)(2,1)}, s32[2,4]{1,0:T(2,128)S(1)}, bf16[2,5,256,128]{3,2,1,0:T(8,128)(2,1)S(1)}, s32[]{:T(128)}, /*index=5*/s32[4]{0:T(128)S(1)}, s32[]{:T(128)}) while((s32[]{:T(128)}, bf16[2,5,2304,128]{3,2,1,0:T(8,128)(2,1)}, s32[2,4]{1,0:T(2,128)S(1)}, bf16[2,5,256,128]{3,2,1,0:T(8,128)(2,1)S(1)}, ...), condition=%wide.while_cond, body=%wide.while_body.sunk | while | flops 163869 | bytes 1638603 | solution.py:158
  280.8 5.7 %dynamic-update-slice.3 = bf16[2,5,2304,128]{3,2,1,0:T(8,128)(2,1)} dynamic-update-slice(bf16[2,5,2304,128]{3,2,1,0:T(8,128)(2,1)} %get-tuple-element.109, bf16[1,5,256,128]{3,2,1,0:T(8,128)(2,1)S(1)} %dynamic-slice_select_fusion.2, s32[]{:T(128)} %bitcast.83, s32[]{:T(128)} %constant.41.clone.1..sunk, s32[]{:T(128)} %bitcast.84, s32[]{:T(128)} %constant.41.clone.1..sunk) | dynamic-update-slice | bytes 655364 | tf_op jit(solution)/shard_map/vmap(vmap())/scatter
  293.4 5.7 %dynamic-update-slice.3 = bf16[2,5,2304,128]{3,2,1,0:T(8,128)(2,1)} dynamic-update-slice(bf16[2,5,2304,128]{3,2,1,0:T(8,128)(2,1)} %get-tuple-element.109, bf16[1,5,256,128]{3,2,1,0:T(8,128)(2,1)S(1)} %dynamic-slice_select_fusion.2, s32[]{:T(128)} %bitcast.83, s32[]{:T(128)} %constant.41.clone.1..sunk, s32[]{:T(128)} %bitcast.84, s32[]{:T(128)} %constant.41.clone.1..sunk) | dynamic-update-slice | bytes 655364 | tf_op jit(solution)/shard_map/vmap(vmap())/scatter
  302.3 15.9 %collective-permute-done.7 = bf16[2,5,288,128]{3,2,1,0:T(8,128)(2,1)} collective-permute-done((bf16[2,5,288,128]{3,2,1,0:T(8,128)(2,1)}, bf16[2,5,288,128]{3,2,1,0:T(8,128)(2,1)}, u32[]{:S(2)}, u32[]{:S(2)}) %collective-permute-start.7) | collective-permute-done | bytes 737312 | tf_op jit(solution)/shard_map/ppermute | solution.py:11
  321.3 29.6 %all-reduce.3.cloned.1.call-done = f32[512,2048]{1,0:T(8,128)} async-done(((f32[512,2048]{1,0:T(8,128)}), f32[512,2048]{1,0:T(8,128)}) %all-reduce.3.cloned.1.call-update) | async-done | bytes 4194320 | tf_op jit(solution)/shard_map/psum | solution.py:150
  350.9 4.2 %fusion.12 = bf16[512,2048]{1,0:T(8,128)(2,1)} fusion(f32[512,2048]{1,0:T(8,128)} %all-reduce.3.cloned.1.call-done, bf16[2,256,2048]{2,1,0:T(8,128)(2,1)S(1)} %copy-done.3), kind=kLoop, calls=%fused_computation.29 | loop fusion | flops 3145728 | bytes 8388608 | tf_op jit(solution)/shard_map/convert_element_type | solution.py:151
  (103 shorter events, 72.9 us)
Async XLA Ops:
  7.2 257.0 %copy-start = (bf16[320,2048]{1,0:T(8,128)(2,1)S(1)}, bf16[320,2048]{1,0:T(8,128)(2,1)}, u32[]{:S(2)}) copy-start(bf16[320,2048]{1,0:T(8,128)(2,1)} %param.17) | copy-start | bytes 3932164
  7.2 2.4 copy-start.4
  9.7 9.8 %copy-start.10 = (s32[16]{0:T(128)S(1)}, s32[16]{0:T(128)}, u32[]{:S(2)}) copy-start(s32[16]{0:T(128)} %param.21) | copy-start | bytes 196
  9.7 9.8 %copy-start.13 = (s32[16]{0:T(128)S(1)}, s32[16]{0:T(128)}, u32[]{:S(2)}) copy-start(s32[16]{0:T(128)} %param.22) | copy-start | bytes 196
  10.7 11.0 %collective-permute-start = (bf16[1,5,256,128]{3,2,1,0:T(8,128)(2,1)}, bf16[1,5,256,128]{3,2,1,0:T(8,128)(2,1)}, u32[]{:S(2)}, u32[]{:S(2)}) collective-permute-start(bf16[1,5,256,128]{3,2,1,0:T(8,128)(2,1)} %get-tuple-element.44), channel_id=1, source_target_pairs={{0,4},{4,0},{8,12},{12,8},{16,20},{20,16},{24,28},{28,24},{1,5},{5... | collective-permute-start | bytes 983048 | tf_op jit(solution)/shard_map/ppermute | solution.py:90
  13.7 23.8 %collective-permute-start.1 = (bf16[1,5,256,128]{3,2,1,0:T(8,128)(2,1)S(1)}, bf16[1,5,256,128]{3,2,1,0:T(8,128)(2,1)}, u32[]{:S(2)}, u32[]{:S(2)}) collective-permute-start(bf16[1,5,256,128]{3,2,1,0:T(8,128)(2,1)S(1)} %get-tuple-element.43), channel_id=1, source_target_pairs={{0,8},{4,12},{8,0},{12,4},{16,24},{20,28},{24,16},{28,20},{1,9},{5... | collective-permute-start | bytes 983048 | tf_op jit(solution)/shard_map/ppermute | solution.py:90
  15.3 26.9 %collective-permute-start.2 = (bf16[1,5,256,128]{3,2,1,0:T(8,128)(2,1)S(1)}, bf16[1,5,256,128]{3,2,1,0:T(8,128)(2,1)}, u32[]{:S(2)}, u32[]{:S(2)}) collective-permute-start(bf16[1,5,256,128]{3,2,1,0:T(8,128)(2,1)S(1)} %get-tuple-element.42), channel_id=1, source_target_pairs={{0,12},{4,8},{8,4},{12,0},{16,28},{20,24},{24,20},{28,16},{1,13},{... | collective-permute-start | bytes 983048 | tf_op jit(solution)/shard_map/ppermute | solution.py:90
  15.3 28.6 %collective-permute-start.3 = (bf16[1,5,256,128]{3,2,1,0:T(8,128)(2,1)S(1)}, bf16[1,5,256,128]{3,2,1,0:T(8,128)(2,1)}, u32[]{:S(2)}, u32[]{:S(2)}) collective-permute-start(bf16[1,5,256,128]{3,2,1,0:T(8,128)(2,1)S(1)} %get-tuple-element.41), channel_id=1, source_target_pairs={{0,16},{4,20},{8,24},{12,28},{16,0},{20,4},{24,8},{28,12},{1,17},{... | collective-permute-start | bytes 983048 | tf_op jit(solution)/shard_map/ppermute | solution.py:90
  18.2 45.1 %collective-permute-start.4 = (bf16[1,5,256,128]{3,2,1,0:T(8,128)(2,1)S(1)}, bf16[1,5,256,128]{3,2,1,0:T(8,128)(2,1)}, u32[]{:S(2)}, u32[]{:S(2)}) collective-permute-start(bf16[1,5,256,128]{3,2,1,0:T(8,128)(2,1)S(1)} %get-tuple-element.40), channel_id=1, source_target_pairs={{0,20},{4,16},{8,28},{12,24},{16,4},{20,0},{24,12},{28,8},{1,21},{... | collective-permute-start | bytes 983048 | tf_op jit(solution)/shard_map/ppermute | solution.py:90
  21.7 43.4 %collective-permute-start.5 = (bf16[1,5,256,128]{3,2,1,0:T(8,128)(2,1)S(1)}, bf16[1,5,256,128]{3,2,1,0:T(8,128)(2,1)S(1)}, u32[]{:S(2)}, u32[]{:S(2)}) collective-permute-start(bf16[1,5,256,128]{3,2,1,0:T(8,128)(2,1)S(1)} %get-tuple-element.46), channel_id=1, source_target_pairs={{0,24},{4,28},{8,16},{12,20},{16,8},{20,12},{24,0},{28,4},{1,25},{... | collective-permute-start | bytes 983048 | tf_op jit(solution)/shard_map/ppermute | solution.py:90
  37.5 28.3 %collective-permute-start.6 = (bf16[1,5,256,128]{3,2,1,0:T(8,128)(2,1)S(1)}, bf16[1,5,256,128]{3,2,1,0:T(8,128)(2,1)S(1)}, u32[]{:S(2)}, u32[]{:S(2)}) collective-permute-start(bf16[1,5,256,128]{3,2,1,0:T(8,128)(2,1)S(1)} %get-tuple-element.39), channel_id=1, source_target_pairs={{0,28},{4,24},{8,20},{12,16},{16,12},{20,8},{24,4},{28,0},{1,29},{... | collective-permute-start | bytes 983048 | tf_op jit(solution)/shard_map/ppermute | solution.py:90
  77.3 128.7 %all-to-all-start = ((bf16[16,5,256,128]{3,2,1,0:T(8,128)(2,1)}), bf16[16,5,256,128]{3,2,1,0:T(8,128)(2,1)}, u32[]{:S(2)}, u32[]{:S(2)}) async-start(bf16[16,5,256,128]{3,2,1,0:T(8,128)(2,1)} %select_select_fusion), calls=%async_computation | async-start | bytes 10485760 | tf_op jit(solution)/shard_map/all_to_all | solution.py:101
  90.8 4.7 %copy-start.2 = (bf16[2,256,2048]{2,1,0:T(8,128)(2,1)S(1)}, bf16[2,256,2048]{2,1,0:T(8,128)(2,1)}, u32[]{:S(2)}) copy-start(bf16[2,256,2048]{2,1,0:T(8,128)(2,1)} %param.13) | copy-start | bytes 6291460
  90.8 260.1 %all-reduce.3.cloned.1.call-start = ((), (), s32[]{:S(2)}) async-start(), calls=%async_computation.1 | async-start | bytes 8388608 | tf_op jit(solution)/shard_map/psum | solution.py:150
  90.9 5.1 %copy-start.16 = (f32[2048]{0:T(1024)S(1)}, f32[2048]{0:T(1024)}, u32[]{:S(2)}) copy-start(f32[2048]{0:T(1024)} %param.14) | copy-start | bytes 24580
  96.0 5.2 %copy-start.14 = (s32[16]{0:T(128)S(1)}, s32[16]{0:T(128)}, u32[]{:S(2)}) copy-start(s32[16]{0:T(128)} %param.23) | copy-start | bytes 196
  102.5 2.8 copy-start.6
  102.5 2.8 copy-start.11
  102.5 2.8 copy-start.12
  210.1 4.2 %copy-start.1 = (bf16[2,5,2048,128]{3,2,1,0:T(8,128)(2,1)}, bf16[2,5,2048,128]{3,2,1,0:T(8,128)(2,1)S(1)}, u32[]{:S(2)}) copy-start(bf16[2,5,2048,128]{3,2,1,0:T(8,128)(2,1)S(1)} %bitcast_select_fusion) | copy-start | bytes 15728644
  257.8 6.4 %copy-start.8 = (bf16[5,64,256]{2,1,0:T(8,128)(2,1)S(1)}, bf16[5,64,256]{2,1,0:T(8,128)(2,1)}, u32[]{:S(2)}) copy-start(bf16[5,64,256]{2,1,0:T(8,128)(2,1)} %fusion.37) | copy-start | bytes 491524
  268.2 5.6 %copy-start.9 = (s32[4]{0:T(128)S(1)}, s32[4]{0:T(128)}, u32[]{:S(2)}) copy-start(s32[4]{0:T(128)} %constant.248) | copy-start | bytes 52
  299.1 51.8 %copy-start.3 = (bf16[2,256,2048]{2,1,0:T(8,128)(2,1)S(1)}, bf16[2,256,2048]{2,1,0:T(8,128)(2,1)}, u32[]{:S(2)}) copy-start(bf16[2,256,2048]{2,1,0:T(8,128)(2,1)} %param.13) | copy-start | bytes 6291460
  301.9 16.3 %collective-permute-start.7 = (bf16[2,5,288,128]{3,2,1,0:T(8,128)(2,1)}, bf16[2,5,288,128]{3,2,1,0:T(8,128)(2,1)}, u32[]{:S(2)}, u32[]{:S(2)}) collective-permute-start(bf16[2,5,288,128]{3,2,1,0:T(8,128)(2,1)} %get-tuple-element.36), channel_id=1, source_target_pairs={{0,4},{4,0},{8,12},{12,8},{16,20},{20,16},{24,28},{28,24},{1,5},{5... | collective-permute-start | bytes 2211848 | tf_op jit(solution)/shard_map/ppermute | solution.py:11
  (3 other events, 2.7 us)
Sparse Core Ops, SparseCore 0:
  267.6 83.3 all-reduce.2
